TPU v7x, 512 devices: a whole 4x4x16 slice. The times are simulated.
512 devices in a mesh: dp: 64 (over x, z), expert: 8 (over y, core).
Axes of the slice: x: 4, y: 4, z: 16, core: 2. Of those that a mesh axis runs over, the one named last changes fastest.
Arguments:
- tokens: bfloat16 [8192, 2048], P('dp'), may hold values from -6 to 6
- routes: int32 [8192, 8], P('dp'), may hold values from 0 to 63, all different within a row; in each aligned block of 128 rows (0 to 127, 128 to 255, ...) at most 16 rows name the same one
- kept_mask: int32 [8192, 8], P('dp'), may hold values from 0 to 1, as said below
- gate_probs: float32 [8192, 8], P('dp'), may hold values from 0.05 to 0.5
- output_grad: bfloat16 [8192, 2048], P('dp'), may hold values from -96 to 96
- w_gate: bfloat16 [64, 2048, 1024], P('dp', None, 'expert'), may hold values from -0.125 to 0.125
- w_up: bfloat16 [64, 2048, 1024], P('dp', None, 'expert'), may hold values from -0.125 to 0.125
- w_down: bfloat16 [64, 1024, 2048], P('dp', 'expert'), may hold values from -0.1875 to 0.1875
Outputs:
- output: bfloat16 [8192, 2048], P('dp', 'expert')
- input_grad: bfloat16 [8192, 2048], P('dp', 'expert')
- grad_gate: bfloat16 [64, 2048, 1024], P('dp', None, 'expert')
- grad_up: bfloat16 [64, 2048, 1024], P('dp', None, 'expert')
- grad_down: bfloat16 [64, 1024, 2048], P('dp', 'expert')
Inputs may be any that keep to these rules, and one draw needn't show every extreme that they name: `routes`: each row names 8 different experts, and the 128 rows of each index of dp name every expert exactly 16 times. `kept_mask`: the share of kept entries varies along the tokens.
All inputs are finite; a program needn't handle non-finite values.
Results may differ from a plain program's by a relative error of at most 0.0064.
Values may be sent and summed in bfloat16 or wider, within the bound.
A program may use at most 64 MiB of HBM per device.

v0:
```python
import functools

import jax
import jax.numpy as jnp
from jax import lax
from jax.sharding import Mesh
from jax.sharding import PartitionSpec as P

DP = ("dp_0", "dp_1")


def by_axis(array, axes):
    return functools.reduce(lax.psum, axes, array)


def side_by_side(arrays, axis, split_dim, concat_dim, along):
    ends, at = ([], 0)
    for a in arrays[:-1]:
        at += a.shape[along]
        ends.append(at)
    both = jnp.concatenate(arrays, axis=along)
    return tuple(
        jnp.split(
            lax.all_to_all(both, axis, split_axis=split_dim, concat_axis=concat_dim, tiled=True),
            ends,
            axis=along,
        )
    )


def from_everyone(array, axis):
    copies = jnp.broadcast_to(array, (lax.axis_size(axis), *array.shape))
    return lax.all_to_all(copies, axis, split_axis=0, concat_axis=0, tiled=True)


def laid_out(parts, dim):
    dims = list(parts.shape[1:])
    dims[dim] *= parts.shape[0]
    return jnp.moveaxis(parts, 0, dim).reshape(dims)


def collect(array, axis, dim):
    parts = from_everyone(array, axis)
    return laid_out(parts, dim)


def sent_together(arrays, axis, dim, along):
    ends, at = ([], 0)
    for a in arrays[:-1]:
        at += a.shape[along]
        ends.append(at)
    both = jnp.concatenate(arrays, axis=along)
    return tuple(jnp.split(lax.all_gather(both, axis, axis=dim, tiled=True), ends, axis=along))


def silu_parts(gate_val):
    sigmoid_val = jax.nn.sigmoid(gate_val)
    return (gate_val * sigmoid_val, sigmoid_val * (1.0 + gate_val * (1.0 - sigmoid_val)))


def slot_layout(routes, experts):
    tok_rows, top_count = routes.shape
    pair_count = tok_rows * top_count
    flat_routes = routes.reshape(pair_count)
    onehot = (flat_routes[:, None] == jnp.arange(experts, dtype=jnp.int32)[None, :]).astype(
        jnp.int32
    )
    before = jnp.cumsum(onehot, axis=0) - onehot
    slot_index = jnp.sum(before * onehot, axis=1)
    capacity = pair_count // experts
    dest_index = flat_routes * capacity + slot_index
    source = (
        jnp.zeros((pair_count,), jnp.int32)
        .at[dest_index]
        .set(jnp.arange(pair_count, dtype=jnp.int32))
    )
    return (dest_index, source, onehot)


def to_experts(rows_in, dp_size, local_experts):
    capacity = rows_in.shape[1]
    width = rows_in.shape[2]
    grouped = rows_in.reshape(dp_size, local_experts, capacity, width)
    return jnp.swapaxes(grouped, 0, 1).reshape(local_experts, dp_size * capacity, width)


def from_experts(values, dp_size):
    local_experts, slot_total, width = values.shape
    capacity = slot_total // dp_size
    grouped = values.reshape(local_experts, dp_size, capacity, width)
    return jnp.swapaxes(grouped, 0, 1).reshape(dp_size * local_experts, capacity, width)


def combine(back_rows, dest_index, factor, tok_rows, top_count):
    width = back_rows.shape[2]
    picked = back_rows.reshape(-1, width)[dest_index].astype(jnp.float32) * factor[:, None]
    return jnp.sum(picked.reshape(tok_rows, top_count, width), axis=1)


def per_device(tokens, routes, kept_mask, gate_probs, output_grad, w_gate, w_up, w_down):
    dp_size = lax.axis_size(DP)
    part_count = lax.axis_size("expert")
    local_experts, model_width, hidden_part = w_gate.shape
    experts = local_experts * dp_size
    tok_rows, top_count = routes.shape
    capacity = tok_rows * top_count // experts
    col_width = model_width // part_count
    dest_index, source, onehot = slot_layout(routes, experts)
    keep_float = kept_mask.reshape(-1).astype(jnp.float32)
    weight_flat = keep_float * gate_probs.reshape(-1)
    src_token = source // top_count
    src_keep = keep_float[source]
    src_weight = weight_flat[source]
    col_start = lax.axis_index("expert") * col_width
    token_src = lax.dynamic_slice_in_dim(tokens, col_start, col_width, 1)
    cot_src = lax.dynamic_slice_in_dim(output_grad, col_start, col_width, 1)
    send_width = token_src.shape[1]
    rows_send = (token_src[src_token].astype(jnp.float32) * src_keep[:, None]).astype(jnp.bfloat16)
    rows_send = rows_send.reshape(experts, capacity, send_width)
    cot_send = (cot_src[src_token].astype(jnp.float32) * src_weight[:, None]).astype(jnp.bfloat16)
    cot_send = cot_send.reshape(experts, capacity, send_width)
    totals = jnp.sum(onehot.astype(jnp.float32) * keep_float[:, None], axis=0)
    totals = by_axis(totals, DP)
    kept_count = lax.dynamic_slice_in_dim(totals, lax.axis_index(DP) * local_experts, local_experts)
    rows_in = lax.all_to_all(rows_send, DP, split_axis=0, concat_axis=0, tiled=True)
    cot_in = lax.all_to_all(cot_send, DP, split_axis=0, concat_axis=0, tiled=True)
    rows_in = lax.all_gather(rows_in, "expert", axis=2, tiled=True)
    cot_in = lax.all_gather(cot_in, "expert", axis=2, tiled=True)
    expert_in = to_experts(rows_in, dp_size, local_experts)
    cot_full = to_experts(cot_in, dp_size, local_experts)
    down_cols = lax.all_to_all(w_down, "expert", split_axis=2, concat_axis=1, tiled=True)
    gate_rows, up_rows = side_by_side((w_gate, w_up), "expert", 1, 2, 0)
    gate_val = jnp.einsum("lsd,ldh->lsh", expert_in, w_gate, preferred_element_type=jnp.float32)
    up_val = jnp.einsum("lsd,ldh->lsh", expert_in, w_up, preferred_element_type=jnp.float32)
    act_val, act_slope = silu_parts(gate_val)
    hidden = (act_val * up_val).astype(jnp.bfloat16)
    expert_out = jnp.einsum(
        "lsh,lhc->lsc", collect(hidden, "expert", 2), down_cols, preferred_element_type=jnp.float32
    ).astype(jnp.bfloat16)
    out_back = lax.all_to_all(
        from_experts(expert_out, dp_size), DP, split_axis=0, concat_axis=0, tiled=True
    )
    output = combine(out_back, dest_index, weight_flat, tok_rows, top_count).astype(jnp.bfloat16)
    d_hidden = jnp.einsum("lsd,lhd->lsh", cot_full, w_down, preferred_element_type=jnp.float32)
    d_gate = (d_hidden * up_val * act_slope).astype(jnp.bfloat16)
    d_up = (d_hidden * act_val).astype(jnp.bfloat16)
    inv_count = (1.0 / jnp.maximum(kept_count, 1.0))[:, None, None]
    grad_down = (
        jnp.einsum("lsh,lsd->lhd", hidden, cot_full, preferred_element_type=jnp.float32) * inv_count
    ).astype(jnp.bfloat16)
    grad_gate = (
        jnp.einsum("lsd,lsh->ldh", expert_in, d_gate, preferred_element_type=jnp.float32)
        * inv_count
    ).astype(jnp.bfloat16)
    grad_up = (
        jnp.einsum("lsd,lsh->ldh", expert_in, d_up, preferred_element_type=jnp.float32) * inv_count
    ).astype(jnp.bfloat16)
    portions = sent_together((d_gate, d_up), "expert", 2, 0)
    running = jnp.einsum("lsh,lch->lsc", portions[0], gate_rows, preferred_element_type=jnp.float32)
    d_rows = (
        running
        + jnp.einsum("lsh,lch->lsc", portions[1], up_rows, preferred_element_type=jnp.float32)
    ).astype(jnp.bfloat16)
    grad_back = lax.all_to_all(
        from_experts(d_rows, dp_size), DP, split_axis=0, concat_axis=0, tiled=True
    )
    input_grad = combine(grad_back, dest_index, keep_float, tok_rows, top_count).astype(
        jnp.bfloat16
    )
    return (output, input_grad, grad_gate, grad_up, grad_down)


def solution(mesh):
    torus = Mesh(mesh.devices.reshape(4, 16, mesh.shape["expert"]), ("dp_0", "dp_1", "expert"))
    return jax.shard_map(
        per_device,
        mesh=torus,
        in_specs=(
            P(DP, None),
            P(DP, None),
            P(DP, None),
            P(DP, None),
            P(DP, None),
            P(DP, None, "expert"),
            P(DP, None, "expert"),
            P(DP, "expert", None),
        ),
        out_specs=(
            P(DP, "expert"),
            P(DP, "expert"),
            P(DP, None, "expert"),
            P(DP, None, "expert"),
            P(DP, "expert", None),
        ),
        check_vma=False,
    )
```

profile of v0, /device:TPU:6, one launch (start us, length us, event | category | flops | bytes accessed | tf_op | source)
XLA Modules:
  0.0 399.1 jit_solution(6085551324650519194)
XLA Ops:
  10.0 18.0 %reduce-window.6 = s32[64,8,128]{2,1,0:T(8,128)S(1)} reduce-window(s32[64,8,128]{2,1,0:T(8,128)S(1)} %fusion.34, s32[]{:T(128)} %constant.17.clone.1), window={size=1x1x128 pad=0_0x0_0x127_0}, to_apply=%region_0.0 | reduce-window | flops 8323072 | bytes 524292 | tf_op jit(solution)/shard_map/reduce-window
  28.7 4.3 %scatter_custom_fusion = s32[1024]{0:T(1024)S(1)} fusion(s32[1024]{0:T(1024)S(1)} %bitcast.119, s32[1024]{0:T(1024)S(1)} %iota.11, s32[]{:T(128)} %constant.17.clone.1), kind=kCustom, calls=%fused_computation.73 | custom fusion | bytes 4100 | tf_op jit(solution)/shard_map/scatter | solution.py:75
  33.0 4.5 %gather_fusion.1 = f32[1024]{0:T(1024)S(1)} fusion(f32[1024]{0:T(1024)S(1)} %convert_element_type.113, s32[1024]{0:T(1024)S(1)} %get-tuple-element.10), kind=kCustom, calls=%fused_computation.1 | custom fusion | bytes 12288 | tf_op jit(solution)/shard_map/gather | solution.py:112
  38.5 3.9 gather_fusion
  42.7 50.4 %all_to_all.55 = bf16[64,16,256]{2,1,0:T(8,128)(2,1)} all-to-all(bf16[64,16,256]{2,1,0:T(8,128)(2,1)S(1)} %fusion.21), channel_id=1, replica_groups=mesh['dp_0'=4,'dp_1'=16,'expert'=8] {'dp_0','dp_1'}, dimensions={0} | all-to-all | bytes 1048576 | tf_op jit(solution)/shard_map/all_to_all | solution.py:125
  93.3 4.5 %gather_fusion.4 = f32[1024]{0:T(1024)S(1)} fusion(f32[1024]{0:T(1024)S(1)} %mul.150, s32[1024]{0:T(1024)S(1)} %get-tuple-element.10), kind=kCustom, calls=%fused_computation.4 | custom fusion | bytes 12288 | tf_op jit(solution)/shard_map/gather | solution.py:113
  97.9 3.9 gather_fusion.3
  102.1 37.6 %all_to_all.56 = bf16[64,16,256]{2,1,0:T(8,128)(2,1)} all-to-all(bf16[64,16,256]{2,1,0:T(8,128)(2,1)S(1)} %fusion.19), channel_id=1, replica_groups=mesh['dp_0'=4,'dp_1'=16,'expert'=8] {'dp_0','dp_1'}, dimensions={0} | all-to-all | bytes 1048576 | tf_op jit(solution)/shard_map/all_to_all | solution.py:126
  143.4 32.5 %all-gather.6.cloned.1.call-done = bf16[64,16,2048]{2,1,0:T(8,128)(2,1)} async-done(((bf16[64,16,256]{2,1,0:T(8,128)(2,1)}), bf16[64,16,2048]{2,1,0:T(8,128)(2,1)}) %all-gather.6.cloned.1.call-update) | async-done | bytes 4194320 | tf_op jit(solution)/shard_map/all_gather | solution.py:128
  183.8 11.5 %reduce = bf16[2048,128]{1,0:T(8,128)(2,1)S(1)} reduce(bf16[2048,1,128]{2,1,0:T(2,128)(2,1)S(1)} %bitcast.108, bf16[]{:T(256)} %broadcast.119), dimensions={1}, to_apply=%bitcast.82.reduce_sub_computation | reduce | bytes 1048578
  195.5 18.9 %all_to_all.57 = bf16[8,2,16384]{2,1,0:T(2,128)(2,1)S(1)} all-to-all(bf16[8,2,16384]{2,1,0:T(2,128)(2,1)S(1)} %reshape.300), channel_id=1, replica_groups=mesh['dp_0'=4,'dp_1'=16,'expert'=8] {'expert'}, dimensions={0} | all-to-all | bytes 1048576 | tf_op jit(solution)/shard_map/all_to_all | solution.py:131
  216.0 4.6 %all-to-all-start.1 = ((bf16[8,1,1024,128]{3,2,1,0:T(8,128)(2,1)}), bf16[8,1,1024,128]{3,2,1,0:T(8,128)(2,1)}, u32[]{:S(2)}, u32[]{:S(2)}) async-start(bf16[8,1,1024,128]{3,2,1,0:T(8,128)(2,1)} %broadcast_in_dim.8), calls=%async_computation.1 | async-start | bytes 4194304 | tf_op jit(solution)/shard_map/all_to_all | solution.py:33
  220.6 8.1 %copy.50 = bf16[1,2048,128]{2,0,1:T(2,128)(2,1)S(1)} copy(bf16[1,2048,128]{2,1,0:T(8,128)(2,1)S(1)} %copy-done.4) | data formatting | bytes 1048576 | tf_op args[5]
  228.7 8.1 %copy.51 = bf16[1,2048,128]{2,0,1:T(2,128)(2,1)S(1)} copy(bf16[1,2048,128]{2,1,0:T(8,128)(2,1)S(1)} %copy-done.3) | data formatting | bytes 1048576 | tf_op args[6]
  240.1 11.8 %all-to-all-done.1 = bf16[8,1,1024,128]{3,2,1,0:T(8,128)(2,1)} async-done(((bf16[8,1,1024,128]{3,2,1,0:T(8,128)(2,1)}), bf16[8,1,1024,128]{3,2,1,0:T(8,128)(2,1)}, u32[]{:S(2)}, u32[]{:S(2)}) %all-to-all-start.1) | async-done | bytes 2097184 | tf_op jit(solution)/shard_map/all_to_all | solution.py:33
  259.5 12.0 %all-to-all-done.5 = bf16[2,2048,128]{2,0,1:T(2,128)(2,1)S(1)} async-done(((bf16[2,2048,128]{2,0,1:T(2,128)(2,1)}), bf16[2,2048,128]{2,0,1:T(2,128)(2,1)S(1)}, u32[]{:S(2)}, u32[]{:S(2)}) %all-to-all-start.5) | async-done | bytes 1048608 | tf_op jit(solution)/shard_map/all_to_all | solution.py:24
  271.5 15.9 %all-to-all-start.3 = ((bf16[64,16,256]{2,1,0:T(8,128)(2,1)}), bf16[64,16,256]{2,1,0:T(8,128)(2,1)S(1)}, u32[]{:S(2)}, u32[]{:S(2)}) async-start(bf16[64,16,256]{2,1,0:T(8,128)(2,1)} %bitcast.14), calls=%async_computation.3 | async-start | bytes 1048576 | tf_op jit(solution)/shard_map/all_to_all | solution.py:140
  292.5 26.1 %all-to-all-done.3 = bf16[64,16,256]{2,1,0:T(8,128)(2,1)S(1)} async-done(((bf16[64,16,256]{2,1,0:T(8,128)(2,1)}), bf16[64,16,256]{2,1,0:T(8,128)(2,1)S(1)}, u32[]{:S(2)}, u32[]{:S(2)}) %all-to-all-start.3) | async-done | bytes 524320 | tf_op jit(solution)/shard_map/all_to_all | solution.py:140
  318.6 6.8 %all-to-all-start.6 = ((bf16[64,16,256]{2,1,0:T(8,128)(2,1)}), bf16[64,16,256]{2,1,0:T(8,128)(2,1)S(1)}, u32[]{:S(2)}, u32[]{:S(2)}) async-start(bf16[64,16,256]{2,1,0:T(8,128)(2,1)} %bitcast.29), calls=%async_computation.6 | async-start | bytes 1048576 | tf_op jit(solution)/shard_map/all_to_all | solution.py:164
  325.7 7.5 %psum.14 = f32[64]{0:T(128)S(1)} all-reduce(f32[64]{0:T(128)S(1)} %fusion.33), channel_id=1, replica_groups=mesh['dp_0'=4,'dp_1'=16,'expert'=8] {'dp_0'}, use_global_device_ids=true, to_apply=%region_7.8 | all-reduce | flops 64 | bytes 512 | tf_op jit(solution)/shard_map/psum | solution.py:13
  333.2 39.8 %psum.15 = f32[64]{0:T(128)S(1)} all-reduce(f32[64]{0:T(128)S(1)} %psum.14), channel_id=1, replica_groups=mesh['dp_0'=4,'dp_1'=16,'expert'=8] {'dp_1'}, use_global_device_ids=true, to_apply=%region_8.9 | all-reduce | flops 64 | bytes 512 | tf_op jit(solution)/shard_map/psum | solution.py:13
  374.6 3.8 fusion.3
  382.6 3.9 gather_fusion.2
  387.6 3.9 gather_fusion.5
  (90 shorter events, 41.4 us)
Async XLA Ops:
  7.2 132.8 %all-gather.4.cloned.1.call-start = ((), (), s32[]{:S(2)}) async-start(), calls=%async_computation.7 | async-start | bytes 4718592 | tf_op jit(solution)/shard_map/all_gather | solution.py:127
  37.5 55.6 %copy-start.9 = (f32[128,8]{0,1:T(8,128)S(1)}, f32[128,8]{0,1:T(8,128)}, u32[]{:S(2)}) copy-start(f32[128,8]{0,1:T(8,128)} %param.11) | copy-start | bytes 12292
  93.1 82.8 %all-gather.6.cloned.1.call-start = ((), (), s32[]{:S(2)}) async-start(), calls=%async_computation.8 | async-start | bytes 4718592 | tf_op jit(solution)/shard_map/all_gather | solution.py:128
  97.9 42.1 %copy-start.3 = (bf16[1,2048,128]{2,1,0:T(8,128)(2,1)S(1)}, bf16[1,2048,128]{2,1,0:T(8,128)(2,1)}, u32[]{:S(2)}) copy-start(bf16[1,2048,128]{2,1,0:T(8,128)(2,1)} %param.14) | copy-start | bytes 1572868
  102.1 73.8 %copy-start.2 = (bf16[1,128,2048]{2,1,0:T(8,128)(2,1)S(1)}, bf16[1,128,2048]{2,1,0:T(8,128)(2,1)}, u32[]{:S(2)}) copy-start(bf16[1,128,2048]{2,1,0:T(8,128)(2,1)} %param.15) | copy-start | bytes 1572868
  139.7 148.4 %all-gather.8.cloned.1.call-start = ((), (), s32[]{:S(2)}) async-start(), calls=%async_computation.9 | async-start | bytes 4718592 | tf_op jit(solution)/shard_map/all_gather | solution.py:53
  143.4 36.1 %copy-start.4 = (bf16[1,2048,128]{2,1,0:T(8,128)(2,1)S(1)}, bf16[1,2048,128]{2,1,0:T(8,128)(2,1)}, u32[]{:S(2)}) copy-start(bf16[1,2048,128]{2,1,0:T(8,128)(2,1)} %param.13) | copy-start | bytes 1572868
  175.9 3.6 copy-start
  180.9 0.7 copy-start.5
  180.9 0.8 copy-start.7
  216.0 35.9 %all-to-all-start.1 = ((bf16[8,1,1024,128]{3,2,1,0:T(8,128)(2,1)}), bf16[8,1,1024,128]{3,2,1,0:T(8,128)(2,1)}, u32[]{:S(2)}, u32[]{:S(2)}) async-start(bf16[8,1,1024,128]{3,2,1,0:T(8,128)(2,1)} %broadcast_in_dim.8), calls=%async_computation.1 | async-start | bytes 4194304 | tf_op jit(solution)/shard_map/all_to_all | solution.py:33
  251.8 19.7 %all-to-all-start.5 = ((bf16[2,2048,128]{2,0,1:T(2,128)(2,1)}), bf16[2,2048,128]{2,0,1:T(2,128)(2,1)S(1)}, u32[]{:S(2)}, u32[]{:S(2)}) async-start(bf16[2,2048,128]{2,0,1:T(2,128)(2,1)} %pad_maximum_fusion), calls=%async_computation.5 | async-start | bytes 2097152 | tf_op jit(solution)/shard_map/all_to_all | solution.py:24
  271.5 47.1 %all-to-all-start.3 = ((bf16[64,16,256]{2,1,0:T(8,128)(2,1)}), bf16[64,16,256]{2,1,0:T(8,128)(2,1)S(1)}, u32[]{:S(2)}, u32[]{:S(2)}) async-start(bf16[64,16,256]{2,1,0:T(8,128)(2,1)} %bitcast.14), calls=%async_computation.3 | async-start | bytes 1048576 | tf_op jit(solution)/shard_map/all_to_all | solution.py:140
  288.1 2.8 copy-start.11
  290.6 34.9 %copy-start.10 = (s32[128,8]{0,1:T(8,128)S(1)}, s32[128,8]{0,1:T(8,128)}, u32[]{:S(2)}) copy-start(s32[128,8]{0,1:T(8,128)} %param.10) | copy-start | bytes 12292
  292.5 85.9 %copy-start.8 = (bf16[1024,128]{1,0:T(8,128)(2,1)S(1)}, bf16[1024,128]{1,0:T(8,128)(2,1)}, u32[]{:S(2)}) copy-start(bf16[1024,128]{1,0:T(8,128)(2,1)} %copy-done.7) | copy-start | bytes 786436
  318.6 69.0 %all-to-all-start.6 = ((bf16[64,16,256]{2,1,0:T(8,128)(2,1)}), bf16[64,16,256]{2,1,0:T(8,128)(2,1)S(1)}, u32[]{:S(2)}, u32[]{:S(2)}) async-start(bf16[64,16,256]{2,1,0:T(8,128)(2,1)} %bitcast.29), calls=%async_computation.6 | async-start | bytes 1048576 | tf_op jit(solution)/shard_map/all_to_all | solution.py:164
  373.0 5.4 %copy-start.1 = (bf16[64,16,2048]{2,1,0:T(8,128)(2,1)S(1)}, bf16[64,16,2048]{2,1,0:T(8,128)(2,1)}, u32[]{:S(2)}) copy-start(bf16[64,16,2048]{2,1,0:T(8,128)(2,1)} %all-gather.4.cloned.1.call-done) | copy-start | bytes 12582916
  374.6 5.9 %copy-start.6 = (bf16[1024,128]{1,0:T(8,128)(2,1)S(1)}, bf16[1024,128]{1,0:T(8,128)(2,1)}, u32[]{:S(2)}) copy-start(bf16[1024,128]{1,0:T(8,128)(2,1)} %copy-done.5) | copy-start | bytes 786436
Sparse Core Ops, SparseCore 0:
  93.2 35.7 all-gather.3
  139.8 36.0 all-gather.5
  182.7 57.1 all-gather.7
where the time goes:
time: 400 us; the launch traced here: 399 us
  blocking collectives  154 us (38%)
  waiting for transfers between devices  82.4 us (21%)
  local copies, waits for them, and re-layouts  54.6 us (14%)
  other arithmetic  37.9 us (9%)
  starting transfers between devices  31.4 us (8%)
  matrix products  23.5 us (6%)
  between operations  15.2 us (4%)
    all_to_all x1, blocking collectives, per_device(): lax.all_to_all(rows_send, DP, split_axis=0, concat_axis=0, tiled=True)  50.4 us
    psum x2, blocking collectives, by_axis(): return functools.reduce(lax.psum, axes, array)  47.3 us
    all_to_all x1, blocking collectives, per_device(): lax.all_to_all(cot_send, DP, split_axis=0, concat_axis=0, tiled=True)  37.6 us
    all_gather x1, waiting for transfers between devices, per_device(): cot_in = lax.all_gather(cot_in, 'expert', axis=2, tiled=True)  32.5 us
    all_to_all x1, waiting for transfers between devices, per_device(): lax.all_to_all(from_experts(expert_out, dp_size), DP, split_axis=0, conca...  26.1 us
    unnamed x33, local copies, waits for them, and re-layouts  20.3 us
    all_to_all x1, blocking collectives, per_device(): lax.all_to_all(w_down, 'expert', split_axis=2, concat_axis=1, tiled=True)  18.9 us
    another operation x3, other arithmetic  18.2 us
  transfers between devices with their start and end apart: 7, of which 4 were waited for; matrix products, arithmetic and copies ran while one was open for 17% of the time, Pallas kernels for 0%

commit v1 on v0

v1 whole, which is shorter than its diff:
```python
import functools

import jax
import jax.numpy as jnp
from jax import lax
from jax.experimental import pallas as pl
from jax.experimental.pallas import tpu as pltpu
from jax.sharding import Mesh
from jax.sharding import PartitionSpec as P

MESH = pl.DeviceIdType.MESH
F32 = jnp.float32
BF16 = jnp.bfloat16

NX, NZ, NY, NC = 4, 16, 4, 2
NF = NY * NC
CH = 64
LAG = 4
NT = (((1,), (1,)), ((), ()))
TN = (((0,), (0,)), ((), ()))


def rdma(src, dst, send_sem, recv_sem, **where):
    return pltpu.make_async_remote_copy(
        src_ref=src,
        dst_ref=dst,
        send_sem=send_sem,
        recv_sem=recv_sem,
        device_id=where,
        device_id_type=MESH,
    )


def rows_of(s, off=0, size=CH):
    return pl.ds(pl.multiple_of(s * CH + off, 16), size)


def mod(v, n):
    return lax.rem(v + 2 * n, n)


def kernel(
    tok,
    grd,
    routes,
    kept,
    probs,
    wg,
    wu,
    wd,
    out,
    ing,
    ggate,
    gup,
    gdown,
    tbuf,
    rbuf,
    stg,
    xc,
    hdu,
    wgu,
    gu,
    dn,
    eo,
    ret,
    psend,
    precv,
    cst,
    crecv,
    local_sem,
    wgt_send,
    wgt_recv,
    z_send,
    z_recv,
    x_send,
    x_recv,
    c_send,
    c_recv,
    ag1_send,
    ag1_y,
    ag1_h,
    ag1_c,
    ag2_send,
    ag2_y,
    ag2_h,
    ag2_c,
    e_send,
    e_recv,
    p_send,
    p_recv,
):
    x = lax.axis_index("x")
    z = lax.axis_index("z")
    y = lax.axis_index("y")
    c = lax.axis_index("c")
    f = y * NC + c
    zp, zm = mod(z + 1, NZ), mod(z - 1, NZ)
    yp, ym, y2 = mod(y + 1, NY), mod(y - 1, NY), mod(y + 2, NY)
    oc = 1 - c
    width = out.shape[1]

    cols = pl.ds(pl.multiple_of(f * width, width), width)
    own_t = pltpu.make_async_copy(tok.at[:, cols], tbuf.at[z, :, pl.ds(0, width)], local_sem.at[0])
    own_g = pltpu.make_async_copy(grd.at[:, cols], tbuf.at[z, :, pl.ds(width, width)], local_sem.at[1])
    own_t.start()
    own_g.start()
    hid = wg.shape[1]
    side_g = pltpu.make_async_copy(wg, wgu.at[:, pl.ds(0, hid)], local_sem.at[2])
    side_u = pltpu.make_async_copy(wu, wgu.at[:, pl.ds(hid, hid)], local_sem.at[3])
    side_g.start()
    side_u.start()

    barrier = pltpu.get_barrier_semaphore()
    for where in [{"z": zp}, {"z": zm}] + [{"x": mod(x + d, NX)} for d in range(1, NX)]:
        pl.semaphore_signal(barrier, inc=1, device_id=where, device_id_type=MESH)
    for d in range(1, NF):
        to = mod(f + d, NF)
        pl.semaphore_signal(
            barrier, inc=1, device_id={"y": to // NC, "c": lax.rem(to, NC)}, device_id_type=MESH
        )

    nexp = NX * NZ
    tok_rows = routes.shape[1]
    rt = routes[...]
    e_iota = lax.broadcasted_iota(jnp.int32, (nexp, tok_rows), 0)
    named = jnp.zeros((nexp, tok_rows), F32)
    for k in range(8):
        named = named + jnp.where(rt[k : k + 1, :] == e_iota, 1.0, 0.0)
    before = lax.broadcasted_iota(jnp.int32, (tok_rows, tok_rows), 0) < lax.broadcasted_iota(
        jnp.int32, (tok_rows, tok_rows), 1
    )
    rank = jnp.dot(
        named.astype(BF16), jnp.where(before, 1.0, 0.0).astype(BF16), preferred_element_type=F32
    )
    kf = kept[...].astype(F32)
    weight = kf * probs[...]
    for k in range(8):
        slot = jnp.sum(jnp.where(rt[k : k + 1, :] == e_iota, rank, 0.0), axis=0, keepdims=True)
        dest = rt[k : k + 1, :].astype(F32) * 16.0 + slot
        rbuf[z, k : k + 1, :] = jnp.where(kf[k : k + 1, :] > 0.0, dest, -1.0)
        rbuf[z, 8 + k : 9 + k, :] = weight[k : k + 1, :]
    cst[...] = jnp.zeros_like(cst)

    pl.semaphore_wait(barrier, 2 + (NX - 1) + (NF - 1))
    own_t.wait()
    own_g.wait()

    def z_copies(direction, s, hop):
        to = zp if direction == 0 else zm
        return [
            rdma(buf.at[s], buf.at[s], z_send.at[direction, i], z_recv.at[direction, i, hop], z=to)
            for i, buf in enumerate((tbuf, rbuf))
        ]

    def z_start(direction, s, hop):
        for copy in z_copies(direction, s, hop):
            copy.start()

    def z_wait(direction, s, hop):
        for copy in z_copies(direction, s, hop):
            copy.wait_recv()

    z_start(0, z, 0)
    z_start(1, z, 0)

    def wblock(ref, b):
        at = pl.ds(pl.multiple_of(b * width, width), width)
        return ref.at[at, :] if ref is not wd else ref.at[:, at]

    def wplace(i, b):
        return (
            gu.at[b, :, pl.ds(0, hid)] if i == 0 else gu.at[b, :, pl.ds(hid, hid)] if i == 1 else dn.at[b]
        )

    for d in range(1, NF):
        to = mod(f + d, NF)
        for i, ref in enumerate((wg, wu, wd)):
            rdma(
                wblock(ref, to),
                wplace(i, f),
                wgt_send.at[i],
                wgt_recv.at[i, f],
                y=to // NC,
                c=lax.rem(to, NC),
            ).start()
    own_w = [
        pltpu.make_async_copy(wblock(ref, f), wplace(i, f), wgt_recv.at[i, f])
        for i, ref in enumerate((wg, wu, wd))
    ]
    for copy in own_w:
        copy.start()

    def selection(s):
        info = rbuf[s]
        r = lax.broadcasted_iota(jnp.int32, (CH, tok_rows), 0)
        name = ((r >> 4) * (NZ * 16) + (r & 15) + z * 16).astype(F32)
        hit = jnp.zeros((CH, tok_rows), F32)
        wgt = jnp.zeros((CH, tok_rows), F32)
        for k in range(8):
            same = info[k : k + 1, :] == name
            hit = hit + jnp.where(same, 1.0, 0.0)
            wgt = wgt + jnp.where(same, info[8 + k : 9 + k, :], 0.0)
        return hit, wgt

    def select_rows(s):
        hit, wgt = selection(s)
        picked = jnp.dot(hit.astype(BF16), tbuf[s], preferred_element_type=F32)
        scale = jnp.sum(wgt, axis=1, keepdims=True)
        stg[s, :, 0:width] = picked[:, :width].astype(BF16)
        stg[s, :, width:] = (picked[:, width:] * scale).astype(BF16)
        cst[...] += hit

    def x_copies(src, dst, send, recv, s):
        def part(v):
            return pl.ds(pl.multiple_of(v * 16, 16), 16)

        mine = pltpu.make_async_copy(src(s, x), dst(s, x), recv.at[s, x])
        others = []
        for d in range(1, NX):
            to = mod(x + d, NX)
            others.append(rdma(src(s, to), dst(s, x), send, recv.at[s, x], x=to))
        return mine, others

    def x_waits(src, dst, send, recv, s):
        pltpu.make_async_copy(src(s, x), dst(s, x), recv.at[s, x]).wait()
        for d in range(1, NX):
            frm = mod(x + d, NX)
            rdma(src(s, frm), dst(s, frm), send, recv.at[s, frm], x=frm).wait_recv()

    def stg_src(s, v):
        return stg.at[s, pl.ds(pl.multiple_of(v * 16, 16), 16), :]

    def xc_dst(s, v):
        return xc.at[f, pl.ds(pl.multiple_of(s * CH + v * 16, 16), 16), :]

    def x_send_rows(s):
        mine, others = x_copies(stg_src, xc_dst, x_send, x_recv, s)
        mine.start()
        for copy in others:
            copy.start()

    def x_wait_rows(s):
        x_waits(stg_src, xc_dst, x_send, x_recv, s)

    def gatherer(buf, send, ysem, hsem, csem):
        def own(s):
            here = buf.at[f, rows_of(s)]
            rdma(here, here, send.at[0], ysem.at[0, s], y=yp).start()
            rdma(here, here, send.at[1], ysem.at[1, s], y=ym).start()
            rdma(here, here, send.at[2], csem.at[0, s], c=oc).start()

        def forward(s):
            for i, (frm, to, off) in enumerate(((ym, yp, 0), (yp, ym, CH // 2))):
                b = frm * NC + c
                whole = buf.at[b, rows_of(s)]
                half = buf.at[b, rows_of(s, off, CH // 2)]
                rdma(whole, whole, send.at[i], ysem.at[i, s], y=frm).wait_recv()
                rdma(half, half, send.at[3 + i], hsem.at[i, s], y=to).start()
                rdma(whole, whole, send.at[5 + i], csem.at[1 + i, s], c=oc).start()

        def halves(s):
            b = y2 * NC + c
            whole = buf.at[b, rows_of(s)]
            for i, frm in enumerate((ym, yp)):
                half = buf.at[b, rows_of(s, i * (CH // 2), CH // 2)]
                rdma(half, half, send.at[3 + i], hsem.at[i, s], y=frm).wait_recv()
            rdma(whole, whole, send.at[7], csem.at[3, s], c=oc).start()

        def other_core(s):
            for i, yy in enumerate((y, ym, yp, y2)):
                whole = buf.at[yy * NC + oc, rows_of(s)]
                rdma(whole, whole, send.at[2], csem.at[i, s], c=oc).wait_recv()

        def drain():
            full = buf.at[f]
            half = buf.at[f, pl.ds(0, NZ * CH // 2)]
            for i in range(8):
                part = half if i in (3, 4) else full
                rdma(part, part, send.at[i], ysem.at[0, 0], c=oc).wait_send()

        return own, forward, halves, other_core, drain

    own1, forward1, halves1, other1, drain1 = gatherer(xc, ag1_send, ag1_y, ag1_h, ag1_c)
    own2, forward2, halves2, other2, drain2 = gatherer(hdu, ag2_send, ag2_y, ag2_h, ag2_c)

    side_g.wait()
    side_u.wait()

    def up_chunks(sa, sb):
        gate_up = jnp.zeros((2 * CH, 2 * hid), F32)
        d_hid = jnp.zeros((2 * CH, hid), F32)
        for b in range(NF):
            xs = jnp.concatenate([xc[b, rows_of(s), 0:width] for s in (sa, sb)], axis=0)
            cs = jnp.concatenate([xc[b, rows_of(s), width : 2 * width] for s in (sa, sb)], axis=0)
            gate_up += jnp.dot(xs, wgu[b * width : (b + 1) * width, :], preferred_element_type=F32)
            d_hid += lax.dot_general(
                cs, wd[:, b * width : (b + 1) * width], NT, preferred_element_type=F32
            )
        gate, up = gate_up[:, :hid], gate_up[:, hid:]
        sig = jax.nn.sigmoid(gate)
        act = gate * sig
        slope = sig * (1.0 + gate * (1.0 - sig))
        hidden = (act * up).astype(BF16)
        d_gate = (d_hid * up * slope).astype(BF16)
        d_up = (d_hid * act).astype(BF16)
        for i, s in enumerate((sa, sb)):
            part = slice(i * CH, (i + 1) * CH)
            hdu[f, rows_of(s), 0:hid] = hidden[part]
            hdu[f, rows_of(s), hid : 2 * hid] = d_gate[part]
            hdu[f, rows_of(s), 2 * hid : 3 * hid] = d_up[part]

    def pair(k):
        return mod(z - k, NZ), mod(z + 1 + k, NZ)

    half_ring = NZ // 2

    def step1(i, carry):
        sa, sb = pair(i)

        @pl.when(i < half_ring)
        def _():
            @pl.when(i >= 1)
            def _():
                z_wait(0, sa, i - 1)

                @pl.when(i <= half_ring - 2)
                def _():
                    z_start(0, sa, i)

            z_wait(1, sb, i)

            @pl.when(i <= half_ring - 2)
            def _():
                z_start(1, sb, i + 1)

            select_rows(sa)
            select_rows(sb)

        @pl.when((i >= 1) & (i < half_ring + 1))
        def _():
            for s in pair(i - 1):
                x_wait_rows(s)
                own1(s)

        @pl.when((i >= 2) & (i < half_ring + 2))
        def _():
            for s in pair(i - 2):
                forward1(s)

        @pl.when((i >= 3) & (i < half_ring + 3))
        def _():
            for s in pair(i - 3):
                halves1(s)

        @pl.when(i < half_ring)
        def _():
            x_send_rows(sa)
            x_send_rows(sb)

        @pl.when(i >= 4)
        def _():
            pa, pb = pair(i - 4)
            other1(pa)
            other1(pb)
            up_chunks(pa, pb)

        return carry

    lax.fori_loop(0, half_ring + LAG, step1, 0)

    def cst_src(s, v):
        return cst.at[pl.ds(pl.multiple_of(v * 16, 16), 16), :]

    def cst_dst(s, v):
        return crecv.at[v]

    c_mine, c_others = x_copies(cst_src, cst_dst, c_send, c_recv, 0)
    c_mine.start()
    for copy in c_others:
        copy.start()
    x_waits(cst_src, cst_dst, c_send, c_recv, 0)
    total = jnp.sum(jnp.sum(crecv[...], axis=0), axis=0, keepdims=True)
    count = jnp.sum(total, axis=1, keepdims=True)
    inv = 1.0 / jnp.maximum(count, 1.0)

    for copy in own_w:
        copy.wait()
    for d in range(1, NF):
        frm = mod(f + d, NF)
        for i, ref in enumerate((wg, wu, wd)):
            rdma(
                wblock(ref, frm),
                wplace(i, frm),
                wgt_send.at[i],
                wgt_recv.at[i, frm],
                y=frm // NC,
                c=lax.rem(frm, NC),
            ).wait_recv()

    def back_pair(m):
        return mod(z + half_ring - m, NZ), mod(z - (half_ring - 1) + m, NZ)

    def down_chunks(sa, sb):
        e_out = jnp.zeros((2 * CH, width), F32)
        d_row = jnp.zeros((2 * CH, width), F32)
        for b in range(NF):
            hs = jnp.concatenate([hdu[b, rows_of(s), 0:hid] for s in (sa, sb)], axis=0)
            ds = jnp.concatenate([hdu[b, rows_of(s), hid : 3 * hid] for s in (sa, sb)], axis=0)
            e_out += jnp.dot(hs, dn[b], preferred_element_type=F32)
            d_row += lax.dot_general(ds, gu[b], NT, preferred_element_type=F32)
        for i, s in enumerate((sa, sb)):
            part = slice(i * CH, (i + 1) * CH)
            eo[s, :, 0:width] = e_out[part].astype(BF16)
            eo[s, :, width:] = d_row[part].astype(BF16)

    def eo_src(s, v):
        return eo.at[s, pl.ds(pl.multiple_of(v * 16, 16), 16), :]

    def ret_dst(s, v):
        return ret.at[s, pl.ds(pl.multiple_of(v * 16, 16), 16), :]

    def contribution(s):
        hit, wgt = selection(s)
        high = wgt.astype(BF16)
        low = (wgt - high.astype(F32)).astype(BF16)
        back_o = ret[s, :, 0:width]
        back_d = ret[s, :, width:]
        part_o = lax.dot_general(
            jnp.concatenate([high, low], axis=0),
            jnp.concatenate([back_o, back_o], axis=0),
            TN,
            preferred_element_type=F32,
        )
        part_d = lax.dot_general(hit.astype(BF16), back_d, TN, preferred_element_type=F32)
        return part_o, part_d

    def p_copy(direction, m):
        to = zp if direction == 0 else zm
        return rdma(
            psend.at[direction, m],
            precv.at[direction, m],
            p_send.at[direction],
            p_recv.at[direction, m],
            z=to,
        )

    def add_and_store(direction, s, m, carried):
        part_o, part_d = contribution(s)
        if carried:
            part_o += precv[direction, m - 1, :, 0:width].astype(F32)
            part_d += precv[direction, m - 1, :, width:].astype(F32)
        psend[direction, m, :, 0:width] = part_o.astype(BF16)
        psend[direction, m, :, width:] = part_d.astype(BF16)

    def grads(b):
        at = pl.ds(pl.multiple_of(b * width, width), width)
        d_gu = lax.dot_general(
            xc[b, :, 0:width], hdu[f, :, hid : 3 * hid], TN, preferred_element_type=F32
        )
        ggate[at, :] = (d_gu[:, :hid] * inv).astype(BF16)
        gup[at, :] = (d_gu[:, hid:] * inv).astype(BF16)
        d_dn = lax.dot_general(
            hdu[f, :, 0:hid], xc[b, :, width : 2 * width], TN, preferred_element_type=F32
        )
        gdown[:, at] = (d_dn * inv).astype(BF16)

    def step2(i, carry):
        @pl.when(i < half_ring)
        def _():
            for s in back_pair(i):
                own2(s)

        @pl.when((i >= 1) & (i < half_ring + 1))
        def _():
            for s in back_pair(i - 1):
                forward2(s)

        @pl.when((i >= 2) & (i < half_ring + 2))
        def _():
            for s in back_pair(i - 2):
                halves2(s)

        @pl.when((i >= 3) & (i < half_ring + 3))
        def _():
            sa, sb = back_pair(i - 3)
            other2(sa)
            other2(sb)
            down_chunks(sa, sb)

        @pl.when((i >= 4) & (i < half_ring + 3))
        def _():
            m = i - 4
            sa, sb = back_pair(m)
            for s in (sa, sb):
                x_waits(eo_src, ret_dst, e_send, e_recv, s)

            @pl.when(m == 0)
            def _():
                add_and_store(0, sa, m, False)
                add_and_store(1, sb, m, False)

            @pl.when(m >= 1)
            def _():
                p_copy(0, m - 1).wait_recv()
                p_copy(1, m - 1).wait_recv()
                add_and_store(0, sa, m, True)
                add_and_store(1, sb, m, True)

            p_copy(0, m).start()
            p_copy(1, m).start()

        @pl.when((i >= 3) & (i < half_ring + 3))
        def _():
            for s in back_pair(i - 3):
                mine, others = x_copies(eo_src, ret_dst, e_send, e_recv, s)
                mine.start()
                for copy in others:
                    copy.start()

        @pl.when(i < half_ring)
        def _():
            grads(i)

        return carry

    lax.fori_loop(0, half_ring + 3, step2, 0)

    last = half_ring - 1
    sa, sb = back_pair(last)
    x_waits(eo_src, ret_dst, e_send, e_recv, sa)
    p_copy(0, last - 1).wait_recv()
    add_and_store(0, sa, last, True)
    p_copy(0, last).start()
    x_waits(eo_src, ret_dst, e_send, e_recv, sb)
    part_o, part_d = contribution(sb)
    p_copy(1, last - 1).wait_recv()
    part_o += precv[1, last - 1, :, 0:width].astype(F32)
    part_d += precv[1, last - 1, :, width:].astype(F32)
    p_copy(0, last).wait_recv()
    out[...] = (part_o + precv[0, last, :, 0:width].astype(F32)).astype(BF16)
    ing[...] = (part_d + precv[0, last, :, width:].astype(F32)).astype(BF16)

    drain1()
    drain2()
    for direction, hops in ((0, half_ring - 1), (1, half_ring)):
        to = zp if direction == 0 else zm
        for i, buf in enumerate((tbuf, rbuf)):
            part = buf.at[pl.ds(0, hops)]
            rdma(part, part, z_send.at[direction, i], z_recv.at[direction, i, 0], z=to).wait_send()
    x_part = NZ * (NX - 1) // NX
    for ref, sem in ((stg, x_send), (eo, e_send)):
        part = ref.at[pl.ds(0, x_part)]
        rdma(part, part, sem, x_recv.at[0, 0], x=mod(x + 1, NX)).wait_send()
    part = crecv.at[pl.ds(0, NX - 1)]
    rdma(part, part, c_send, c_recv.at[0, 0], x=mod(x + 1, NX)).wait_send()
    for direction, hops in ((0, half_ring), (1, half_ring - 1)):
        part = psend.at[direction, pl.ds(0, hops)]
        to = zp if direction == 0 else zm
        rdma(part, part, p_send.at[direction], p_recv.at[direction, 0], z=to).wait_send()
    for i, ref in enumerate((wg, wu, wd)):
        at = pl.ds(0, (NF - 1) * width)
        part = ref.at[at, :] if i < 2 else ref.at[:, at]
        rdma(part, part, wgt_send.at[i], wgt_recv.at[i, 0], c=oc).wait_send()


def per_device(tokens, routes, kept_mask, gate_probs, output_grad, w_gate, w_up, w_down):
    tok_rows, model = tokens.shape
    width = model // NF
    hid = w_gate.shape[2]
    wg, wu, wd = w_gate[0], w_up[0], w_down[0]
    vmem = pl.BlockSpec(memory_space=pltpu.VMEM)
    hbm = pl.BlockSpec(memory_space=pl.ANY)
    dma = pltpu.SemaphoreType.DMA
    gather_sems = [dma((8,)), dma((2, NZ)), dma((2, NZ)), dma((4, NZ))]
    outs = pl.pallas_call(
        kernel,
        out_shape=(
            jax.ShapeDtypeStruct((tok_rows, width), BF16),
            jax.ShapeDtypeStruct((tok_rows, width), BF16),
            jax.ShapeDtypeStruct(wg.shape, BF16),
            jax.ShapeDtypeStruct(wu.shape, BF16),
            jax.ShapeDtypeStruct(wd.shape, BF16),
        ),
        in_specs=[hbm, hbm] + [vmem] * 6,
        out_specs=[vmem] * 5,
        scratch_shapes=[
            pltpu.VMEM((NZ, tok_rows, 2 * width), BF16),
            pltpu.VMEM((NZ, 16, tok_rows), F32),
            pltpu.VMEM((NZ, CH, 2 * width), BF16),
            pltpu.VMEM((NF, NZ * CH, 2 * width), BF16),
            pltpu.VMEM((NF, NZ * CH, 3 * hid), BF16),
            pltpu.VMEM((model, 2 * hid), BF16),
            pltpu.VMEM((NF, width, 2 * hid), BF16),
            pltpu.VMEM((NF, hid, width), BF16),
            pltpu.VMEM((NZ, CH, 2 * width), BF16),
            pltpu.VMEM((NZ, CH, 2 * width), BF16),
            pltpu.VMEM((2, NZ // 2, tok_rows, 2 * width), BF16),
            pltpu.VMEM((2, NZ // 2, tok_rows, 2 * width), BF16),
            pltpu.VMEM((CH, tok_rows), F32),
            pltpu.VMEM((NX, 16, tok_rows), F32),
            dma((4,)),
            dma((3,)),
            dma((3, NF)),
            dma((2, 2)),
            dma((2, 2, NZ // 2)),
            dma(()),
            dma((NZ, NX)),
            dma(()),
            dma((1, NX)),
            *gather_sems,
            *gather_sems,
            dma(()),
            dma((NZ, NX)),
            dma((2,)),
            dma((2, NZ // 2)),
        ],
        compiler_params=pltpu.CompilerParams(
            collective_id=0, has_side_effects=True, vmem_limit_bytes=56 * 1024 * 1024
        ),
    )(tokens, output_grad, routes.T, kept_mask.T, gate_probs.T, wg, wu, wd)
    output, input_grad, g_gate, g_up, g_down = outs
    return output, input_grad, g_gate[None], g_up[None], g_down[None]


def solution(mesh):
    torus = Mesh(mesh.devices.reshape(NX, NZ, NY, NC), ("x", "z", "y", "c"))
    dp, expert = ("x", "z"), ("y", "c")
    return jax.shard_map(
        per_device,
        mesh=torus,
        in_specs=(
            P(dp, None),
            P(dp, None),
            P(dp, None),
            P(dp, None),
            P(dp, None),
            P(dp, None, expert),
            P(dp, None, expert),
            P(dp, expert, None),
        ),
        out_specs=(
            P(dp, expert),
            P(dp, expert),
            P(dp, None, expert),
            P(dp, None, expert),
            P(dp, expert, None),
        ),
        check_vma=False,
    )
```

time: 400 us -> 149 us (0.37)
  blocking collectives: 154 us -> 0 us
  Pallas kernels: 0 us -> 141 us
  waiting for transfers between devices: 82.4 us -> 0 us
  local copies, waits for them, and re-layouts: 54.6 us -> 6.09 us
  other arithmetic: 37.9 us -> 0 us
  starting transfers between devices: 31.4 us -> 0 us
  matrix products: 23.5 us -> 0 us
  between operations: 15.2 us -> 0.65 us
    pallas_call x0 -> x1, Pallas kernels: none -> 141 us  [per_device(): pl.pallas_call(kernel, out_shape=(jax.ShapeDtypeStruct((tok_rows, width),...]
    all_to_all x3 -> x0, blocking collectives: 107 us -> none  [the longest x1 50.4 us: per_device(): lax.all_to_all(rows_send, DP, split_axis=0, concat_axis=0, tiled=True)]
    all_to_all x4 -> x0, waiting for transfers between devices: 49.9 us -> none  [the longest x1 26.1 us: per_device(): lax.all_to_all(from_experts(expert_out, dp_size), DP, split_axis=0, conca...]
    psum x2 -> x0, blocking collectives: 47.3 us -> none  [by_axis(): return functools.reduce(lax.psum, axes, array)]
    all_gather x3 -> x0, waiting for transfers between devices: 32.5 us -> none  [the longest x1 32.5 us: per_device(): cot_in = lax.all_gather(cot_in, 'expert', axis=2, tiled=True)]
    all_to_all x4 -> x0, starting transfers between devices: 31.1 us -> none  [the longest x1 15.9 us: per_device(): lax.all_to_all(from_experts(expert_out, dp_size), DP, split_axis=0, conca...]
    gather x6 -> x0, local copies, waits for them, and re-layouts: 24.8 us -> none  [the longest x2 7.87 us: combine(): back_rows.reshape(-1, width)[dest_index].astype(jnp.float32)]
    dot_general x9 -> x0, matrix products: 23.5 us -> none  [the longest x1 3.77 us: per_device(): jnp.einsum('lsh,lsd->lhd', hidden, cot_full, preferred_element_type=jnp.f...]
  transfers between devices with their start and end apart: 7 -> 0, of which waited for: 4 -> 0; matrix products, arithmetic and copies ran while one was open for 17% -> 0% of each run, Pallas kernels for 0% -> 0%
where the time goes in v1:
time: 149 us; the launch traced here: 147 us
  Pallas kernels  141 us (95%)
  local copies, waits for them, and re-layouts  6.09 us (4%)
    pallas_call x1, Pallas kernels, per_device(): pl.pallas_call(kernel, out_shape=(jax.ShapeDtypeStruct((tok_rows, width),...  141 us
    unnamed x11, local copies, waits for them, and re-layouts  6.09 us

profile of v1, /device:TPU:6, one launch (start us, length us, event | category | flops | bytes accessed | tf_op | source)
XLA Modules:
  0.0 147.5 jit_solution(17256986297976365890)
XLA Ops:
  0.6 140.7 %shard_map.119 = (bf16[128,256]{1,0:T(8,128)(2,1)}, bf16[128,256]{1,0:T(8,128)(2,1)}, bf16[2048,128]{1,0:T(8,128)(2,1)}, bf16[2048,128]{1,0:T(8,128)(2,1)}, bf16[128,2048]{1,0:T(8,128)(2,1)}) custom-call(bf16[128,2048]{1,0:T(8,128)(2,1)} %tok.1, bf16[128,2048]{1,0:T(8,128)(2,1)} %grd.1, s32[8,128]{1,0:T(8,128)} %bitcast.15, s32[8,128]{1,0:T(8,128)} %bitcast.16, ...), custom_call_target="tpu_custom_call" | custom-call | tf_op jit(solution)/shard_map/pallas_call | solution.py:575
  141.4 0.0 copy-start.2
  141.4 1.5 %copy.18 = bf16[128,256]{1,0:T(8,128)(2,1)} copy(bf16[128,256]{1,0:T(8,128)(2,1)} %get-tuple-element.20) | data formatting | bytes 131072
  142.9 0.0 copy-done.2
  142.9 0.6 copy.19
  143.5 0.0 copy-start.1
  143.5 1.9 %copy.20 = bf16[1,2048,128]{2,1,0:T(8,128)(2,1)} copy(bf16[1,2048,128]{2,1,0:T(8,128)(2,1)} %bitcast.14) | data formatting | bytes 1048576
  145.4 0.0 copy-done.1
  145.4 0.0 copy-start
  145.4 0.8 copy.21
  146.2 0.4 copy-done
  146.7 0.8 copy.22
Async XLA Ops:
  141.4 1.5 %copy-start.2 = (bf16[128,256]{1,0:T(8,128)(2,1)S(1)}, bf16[128,256]{1,0:T(8,128)(2,1)}, u32[]{:S(2)}) copy-start(bf16[128,256]{1,0:T(8,128)(2,1)} %get-tuple-element.21) | copy-start | bytes 196612
  143.5 1.9 %copy-start.1 = (bf16[2048,128]{1,0:T(8,128)(2,1)S(1)}, bf16[2048,128]{1,0:T(8,128)(2,1)}, u32[]{:S(2)}) copy-start(bf16[2048,128]{1,0:T(8,128)(2,1)} %get-tuple-element.13) | copy-start | bytes 1572868
  145.4 1.2 copy-start

commit v2 on v1

--- a/solution.py
+++ b/solution.py
@@ -16,7 +16,7 @@
 NF = NY * NC
 CH = 64
 LAG = 4
-NT = (((1,), (1,)), ((), ()))
+EARLY = 1
 TN = (((0,), (0,)), ((), ()))
 
 
@@ -42,9 +42,9 @@
 def kernel(
     tok,
     grd,
-    routes,
-    kept,
-    probs,
+    routes_h,
+    kept_h,
+    probs_h,
     wg,
     wu,
     wd,
@@ -67,7 +67,19 @@
     precv,
     cst,
     crecv,
+    wdv,
+    gg,
+    gdn,
+    inv_ref,
+    pick_o,
+    pick_d,
+    wdt,
+    gut,
+    routes,
+    kept,
+    probs,
     local_sem,
+    grad_sem,
     wgt_send,
     wgt_recv,
     z_send,
@@ -102,13 +114,22 @@
     cols = pl.ds(pl.multiple_of(f * width, width), width)
     own_t = pltpu.make_async_copy(tok.at[:, cols], tbuf.at[z, :, pl.ds(0, width)], local_sem.at[0])
     own_g = pltpu.make_async_copy(grd.at[:, cols], tbuf.at[z, :, pl.ds(width, width)], local_sem.at[1])
+    infos = [
+        pltpu.make_async_copy(a, b, local_sem.at[5 + i])
+        for i, (a, b) in enumerate(((routes_h, routes), (kept_h, kept), (probs_h, probs)))
+    ]
+    for copy in infos:
+        copy.start()
     own_t.start()
     own_g.start()
     hid = wg.shape[1]
-    side_g = pltpu.make_async_copy(wg, wgu.at[:, pl.ds(0, hid)], local_sem.at[2])
-    side_u = pltpu.make_async_copy(wu, wgu.at[:, pl.ds(hid, hid)], local_sem.at[3])
-    side_g.start()
-    side_u.start()
+    loads = [
+        pltpu.make_async_copy(wg, wgu.at[:, pl.ds(0, hid)], local_sem.at[2]),
+        pltpu.make_async_copy(wu, wgu.at[:, pl.ds(hid, hid)], local_sem.at[3]),
+        pltpu.make_async_copy(wd, wdv, local_sem.at[4]),
+    ]
+    for copy in loads:
+        copy.start()
 
     barrier = pltpu.get_barrier_semaphore()
     for where in [{"z": zp}, {"z": zm}] + [{"x": mod(x + d, NX)} for d in range(1, NX)]:
@@ -121,6 +142,8 @@
 
     nexp = NX * NZ
     tok_rows = routes.shape[1]
+    for copy in infos:
+        copy.wait()
     rt = routes[...]
     e_iota = lax.broadcasted_iota(jnp.int32, (nexp, tok_rows), 0)
     named = jnp.zeros((nexp, tok_rows), F32)
@@ -147,18 +170,26 @@
 
     def z_copies(direction, s, hop):
         to = zp if direction == 0 else zm
+        half = tok_rows // 2
+        parts = [rbuf.at[s]] + [tbuf.at[s, pl.ds(i * half, half), :] for i in range(2)]
         return [
-            rdma(buf.at[s], buf.at[s], z_send.at[direction, i], z_recv.at[direction, i, hop], z=to)
-            for i, buf in enumerate((tbuf, rbuf))
+            rdma(part, part, z_send.at[direction, min(i, 1)], z_recv.at[direction, i, hop], z=to)
+            for i, part in enumerate(parts)
         ]
 
     def z_start(direction, s, hop):
         for copy in z_copies(direction, s, hop):
             copy.start()
 
-    def z_wait(direction, s, hop):
-        for copy in z_copies(direction, s, hop):
-            copy.wait_recv()
+    def z_pass(direction, s, hop, onward, which):
+        arrived = z_copies(direction, s, hop)
+        following = z_copies(direction, s, hop + 1)
+        for came, goes in zip(arrived[which], following[which]):
+            came.wait_recv()
+
+            @pl.when(onward)
+            def _():
+                goes.start()
 
     z_start(0, z, 0)
     z_start(1, z, 0)
@@ -209,6 +240,10 @@
         stg[s, :, 0:width] = picked[:, :width].astype(BF16)
         stg[s, :, width:] = (picked[:, width:] * scale).astype(BF16)
         cst[...] += hit
+        high = wgt.astype(BF16).astype(F32)
+        turned = jnp.transpose(jnp.concatenate([high, wgt - high, hit, hit], axis=0))
+        pick_o[s] = turned[:, : 2 * CH].astype(BF16)
+        pick_d[s] = turned[:, 2 * CH : 3 * CH].astype(BF16)
 
     def x_copies(src, dst, send, recv, s):
         def part(v):
@@ -283,8 +318,11 @@
     own1, forward1, halves1, other1, drain1 = gatherer(xc, ag1_send, ag1_y, ag1_h, ag1_c)
     own2, forward2, halves2, other2, drain2 = gatherer(hdu, ag2_send, ag2_y, ag2_h, ag2_c)
 
-    side_g.wait()
-    side_u.wait()
+    for copy in loads:
+        copy.wait()
+    for b in range(NF):
+        at = slice(b * width, (b + 1) * width)
+        wdt[at, :] = jnp.transpose(wdv[:, at].astype(F32)).astype(BF16)
 
     def up_chunks(sa, sb):
         gate_up = jnp.zeros((2 * CH, 2 * hid), F32)
@@ -293,9 +331,7 @@
             xs = jnp.concatenate([xc[b, rows_of(s), 0:width] for s in (sa, sb)], axis=0)
             cs = jnp.concatenate([xc[b, rows_of(s), width : 2 * width] for s in (sa, sb)], axis=0)
             gate_up += jnp.dot(xs, wgu[b * width : (b + 1) * width, :], preferred_element_type=F32)
-            d_hid += lax.dot_general(
-                cs, wd[:, b * width : (b + 1) * width], NT, preferred_element_type=F32
-            )
+            d_hid += jnp.dot(cs, wdt[b * width : (b + 1) * width, :], preferred_element_type=F32)
         gate, up = gate_up[:, :hid], gate_up[:, hid:]
         sig = jax.nn.sigmoid(gate)
         act = gate * sig
@@ -314,27 +350,38 @@
 
     half_ring = NZ // 2
 
+    def weights_wait():
+        for copy in own_w:
+            copy.wait()
+        for d in range(1, NF):
+            frm = mod(f + d, NF)
+            for i, ref in enumerate((wg, wu, wd)):
+                rdma(
+                    wblock(ref, frm),
+                    wplace(i, frm),
+                    wgt_send.at[i],
+                    wgt_recv.at[i, frm],
+                    y=frm // NC,
+                    c=lax.rem(frm, NC),
+                ).wait_recv()
+
+    def turn(b):
+        gut[b] = jnp.transpose(gu[b].astype(F32)).astype(BF16)
+
     def step1(i, carry):
         sa, sb = pair(i)
-
-        @pl.when(i < half_ring)
-        def _():
-            @pl.when(i >= 1)
+        onward = i <= half_ring - 2
+
+        def z_step(which):
+            @pl.when(i < half_ring)
             def _():
-                z_wait(0, sa, i - 1)
-
-                @pl.when(i <= half_ring - 2)
+                @pl.when(i >= 1)
                 def _():
-                    z_start(0, sa, i)
-
-            z_wait(1, sb, i)
-
-            @pl.when(i <= half_ring - 2)
-            def _():
-                z_start(1, sb, i + 1)
-
-            select_rows(sa)
-            select_rows(sb)
+                    z_pass(0, sa, i - 1, onward, which)
+
+                z_pass(1, sb, i, onward, which)
+
+        z_step(slice(0, 2))
 
         @pl.when((i >= 1) & (i < half_ring + 1))
         def _():
@@ -347,15 +394,28 @@
             for s in pair(i - 2):
                 forward1(s)
 
+        z_step(slice(2, 3))
+
+        @pl.when(i < half_ring)
+        def _():
+            select_rows(sa)
+            select_rows(sb)
+            x_send_rows(sa)
+            x_send_rows(sb)
+
         @pl.when((i >= 3) & (i < half_ring + 3))
         def _():
             for s in pair(i - 3):
                 halves1(s)
 
-        @pl.when(i < half_ring)
-        def _():
-            x_send_rows(sa)
-            x_send_rows(sb)
+        @pl.when(i == half_ring)
+        def _():
+            weights_wait()
+
+        @pl.when(i >= half_ring)
+        def _():
+            for j in range(2):
+                turn((i - half_ring) * 2 + j)
 
         @pl.when(i >= 4)
         def _():
@@ -364,6 +424,11 @@
             other1(pb)
             up_chunks(pa, pb)
 
+            @pl.when(i >= half_ring + LAG - EARLY)
+            def _():
+                own2(pa)
+                own2(pb)
+
         return carry
 
     lax.fori_loop(0, half_ring + LAG, step1, 0)
@@ -378,24 +443,12 @@
     c_mine.start()
     for copy in c_others:
         copy.start()
-    x_waits(cst_src, cst_dst, c_send, c_recv, 0)
-    total = jnp.sum(jnp.sum(crecv[...], axis=0), axis=0, keepdims=True)
-    count = jnp.sum(total, axis=1, keepdims=True)
-    inv = 1.0 / jnp.maximum(count, 1.0)
-
-    for copy in own_w:
-        copy.wait()
-    for d in range(1, NF):
-        frm = mod(f + d, NF)
-        for i, ref in enumerate((wg, wu, wd)):
-            rdma(
-                wblock(ref, frm),
-                wplace(i, frm),
-                wgt_send.at[i],
-                wgt_recv.at[i, frm],
-                y=frm // NC,
-                c=lax.rem(frm, NC),
-            ).wait_recv()
+
+    def count_rows():
+        x_waits(cst_src, cst_dst, c_send, c_recv, 0)
+        total = jnp.sum(jnp.sum(crecv[...], axis=0), axis=0, keepdims=True)
+        count = jnp.sum(total, axis=1, keepdims=True)
+        inv_ref[...] = jnp.broadcast_to(1.0 / jnp.maximum(count, 1.0), inv_ref.shape)
 
     def back_pair(m):
         return mod(z + half_ring - m, NZ), mod(z - (half_ring - 1) + m, NZ)
@@ -407,7 +460,7 @@
             hs = jnp.concatenate([hdu[b, rows_of(s), 0:hid] for s in (sa, sb)], axis=0)
             ds = jnp.concatenate([hdu[b, rows_of(s), hid : 3 * hid] for s in (sa, sb)], axis=0)
             e_out += jnp.dot(hs, dn[b], preferred_element_type=F32)
-            d_row += lax.dot_general(ds, gu[b], NT, preferred_element_type=F32)
+            d_row += jnp.dot(ds, gut[b], preferred_element_type=F32)
         for i, s in enumerate((sa, sb)):
             part = slice(i * CH, (i + 1) * CH)
             eo[s, :, 0:width] = e_out[part].astype(BF16)
@@ -419,132 +472,138 @@
     def ret_dst(s, v):
         return ret.at[s, pl.ds(pl.multiple_of(v * 16, 16), 16), :]
 
-    def contribution(s):
-        hit, wgt = selection(s)
-        high = wgt.astype(BF16)
-        low = (wgt - high.astype(F32)).astype(BF16)
-        back_o = ret[s, :, 0:width]
-        back_d = ret[s, :, width:]
-        part_o = lax.dot_general(
-            jnp.concatenate([high, low], axis=0),
-            jnp.concatenate([back_o, back_o], axis=0),
-            TN,
-            preferred_element_type=F32,
+    def share(kind, s):
+        if kind == 1:
+            return jnp.dot(pick_d[s], ret[s, :, width:], preferred_element_type=F32)
+        back = ret[s, :, 0:width]
+        return jnp.dot(
+            pick_o[s], jnp.concatenate([back, back], axis=0), preferred_element_type=F32
         )
-        part_d = lax.dot_general(hit.astype(BF16), back_d, TN, preferred_element_type=F32)
-        return part_o, part_d
-
-    def p_copy(direction, m):
+
+    def p_copy(direction, kind, m):
         to = zp if direction == 0 else zm
         return rdma(
-            psend.at[direction, m],
-            precv.at[direction, m],
+            psend.at[direction, m, kind],
+            precv.at[direction, m, kind],
             p_send.at[direction],
-            p_recv.at[direction, m],
+            p_recv.at[direction, m, kind],
             z=to,
         )
 
-    def add_and_store(direction, s, m, carried):
-        part_o, part_d = contribution(s)
-        if carried:
-            part_o += precv[direction, m - 1, :, 0:width].astype(F32)
-            part_d += precv[direction, m - 1, :, width:].astype(F32)
-        psend[direction, m, :, 0:width] = part_o.astype(BF16)
-        psend[direction, m, :, width:] = part_d.astype(BF16)
+    def pass_on(direction, kind, s, m):
+        part = share(kind, s)
+
+        @pl.when(m == 0)
+        def _():
+            psend[direction, m, kind] = part.astype(BF16)
+
+        @pl.when(m >= 1)
+        def _():
+            before_m = jnp.maximum(m - 1, 0)
+            p_copy(direction, kind, before_m).wait_recv()
+            came = precv[direction, before_m, kind].astype(F32)
+            psend[direction, m, kind] = (part + came).astype(BF16)
+
+        p_copy(direction, kind, m).start()
+
+    def grad_out(b):
+        at = pl.ds(pl.multiple_of(b * width, width), width)
+        return [
+            pltpu.make_async_copy(gg.at[at, pl.ds(0, hid)], ggate.at[at, :], grad_sem.at[0]),
+            pltpu.make_async_copy(gg.at[at, pl.ds(hid, hid)], gup.at[at, :], grad_sem.at[1]),
+            pltpu.make_async_copy(gdn.at[:, at], gdown.at[:, at], grad_sem.at[2]),
+        ]
 
     def grads(b):
         at = pl.ds(pl.multiple_of(b * width, width), width)
+        inv = inv_ref[0:1, 0:1]
         d_gu = lax.dot_general(
             xc[b, :, 0:width], hdu[f, :, hid : 3 * hid], TN, preferred_element_type=F32
         )
-        ggate[at, :] = (d_gu[:, :hid] * inv).astype(BF16)
-        gup[at, :] = (d_gu[:, hid:] * inv).astype(BF16)
+        gg[at, :] = (d_gu * inv).astype(BF16)
         d_dn = lax.dot_general(
             hdu[f, :, 0:hid], xc[b, :, width : 2 * width], TN, preferred_element_type=F32
         )
-        gdown[:, at] = (d_dn * inv).astype(BF16)
+        gdn[:, at] = (d_dn * inv).astype(BF16)
 
     def step2(i, carry):
+        def pass_kind(kind):
+            @pl.when(i >= 3)
+            def _():
+                m = i - 3
+                chunks = back_pair(m)
+                if kind == 0:
+                    for s in chunks:
+                        x_waits(eo_src, ret_dst, e_send, e_recv, s)
+                for direction in range(2):
+                    pass_on(direction, kind, chunks[direction], m)
+
+        @pl.when(i < half_ring - EARLY)
+        def _():
+            for s in back_pair(i + EARLY):
+                own2(s)
+
+        pass_kind(0)
+
         @pl.when(i < half_ring)
         def _():
             for s in back_pair(i):
-                own2(s)
-
-        @pl.when((i >= 1) & (i < half_ring + 1))
-        def _():
-            for s in back_pair(i - 1):
                 forward2(s)
 
-        @pl.when((i >= 2) & (i < half_ring + 2))
-        def _():
-            for s in back_pair(i - 2):
-                halves2(s)
-
-        @pl.when((i >= 3) & (i < half_ring + 3))
-        def _():
-            sa, sb = back_pair(i - 3)
-            other2(sa)
-            other2(sb)
-            down_chunks(sa, sb)
-
-        @pl.when((i >= 4) & (i < half_ring + 3))
-        def _():
-            m = i - 4
-            sa, sb = back_pair(m)
-            for s in (sa, sb):
-                x_waits(eo_src, ret_dst, e_send, e_recv, s)
-
-            @pl.when(m == 0)
-            def _():
-                add_and_store(0, sa, m, False)
-                add_and_store(1, sb, m, False)
-
-            @pl.when(m >= 1)
-            def _():
-                p_copy(0, m - 1).wait_recv()
-                p_copy(1, m - 1).wait_recv()
-                add_and_store(0, sa, m, True)
-                add_and_store(1, sb, m, True)
-
-            p_copy(0, m).start()
-            p_copy(1, m).start()
-
-        @pl.when((i >= 3) & (i < half_ring + 3))
-        def _():
-            for s in back_pair(i - 3):
+        @pl.when(i >= 2)
+        def _():
+            chunks = back_pair(i - 2)
+            for s in chunks:
+                other2(s)
+            down_chunks(*chunks)
+            for s in chunks:
                 mine, others = x_copies(eo_src, ret_dst, e_send, e_recv, s)
                 mine.start()
                 for copy in others:
                     copy.start()
 
+        @pl.when((i >= 1) & (i < half_ring + 1))
+        def _():
+            for s in back_pair(i - 1):
+                halves2(s)
+
+        pass_kind(1)
+
+        @pl.when(i == 0)
+        def _():
+            count_rows()
+
+        @pl.when((i >= 1) & (i < half_ring + 1))
+        def _():
+            for copy in grad_out(i - 1):
+                copy.start()
+
         @pl.when(i < half_ring)
         def _():
             grads(i)
 
         return carry
 
-    lax.fori_loop(0, half_ring + 3, step2, 0)
+    lax.fori_loop(0, half_ring + 2, step2, 0)
 
     last = half_ring - 1
     sa, sb = back_pair(last)
     x_waits(eo_src, ret_dst, e_send, e_recv, sa)
-    p_copy(0, last - 1).wait_recv()
-    add_and_store(0, sa, last, True)
-    p_copy(0, last).start()
+    for kind in range(2):
+        pass_on(0, kind, sa, jnp.int32(last))
     x_waits(eo_src, ret_dst, e_send, e_recv, sb)
-    part_o, part_d = contribution(sb)
-    p_copy(1, last - 1).wait_recv()
-    part_o += precv[1, last - 1, :, 0:width].astype(F32)
-    part_d += precv[1, last - 1, :, width:].astype(F32)
-    p_copy(0, last).wait_recv()
-    out[...] = (part_o + precv[0, last, :, 0:width].astype(F32)).astype(BF16)
-    ing[...] = (part_d + precv[0, last, :, width:].astype(F32)).astype(BF16)
+    for kind, ref in enumerate((out, ing)):
+        part = share(kind, sb)
+        p_copy(1, kind, last - 1).wait_recv()
+        part += precv[1, last - 1, kind].astype(F32)
+        p_copy(0, kind, last).wait_recv()
+        ref[...] = (part + precv[0, last, kind].astype(F32)).astype(BF16)
 
     drain1()
     drain2()
     for direction, hops in ((0, half_ring - 1), (1, half_ring)):
         to = zp if direction == 0 else zm
-        for i, buf in enumerate((tbuf, rbuf)):
+        for i, buf in enumerate((rbuf, tbuf)):
             part = buf.at[pl.ds(0, hops)]
             rdma(part, part, z_send.at[direction, i], z_recv.at[direction, i, 0], z=to).wait_send()
     x_part = NZ * (NX - 1) // NX
@@ -561,6 +620,22 @@
         at = pl.ds(0, (NF - 1) * width)
         part = ref.at[at, :] if i < 2 else ref.at[:, at]
         rdma(part, part, wgt_send.at[i], wgt_recv.at[i, 0], c=oc).wait_send()
+    pltpu.make_async_copy(gg.at[:, pl.ds(0, hid)], ggate, grad_sem.at[0]).wait()
+    pltpu.make_async_copy(gg.at[:, pl.ds(hid, hid)], gup, grad_sem.at[1]).wait()
+    pltpu.make_async_copy(gdn, gdown, grad_sem.at[2]).wait()
+
+
+def put_out(n, *refs):
+    srcs, dsts, bufs, sems = refs[:n], refs[n : 2 * n], refs[2 * n : 3 * n], refs[3 * n]
+    ins = [pltpu.make_async_copy(srcs[i], bufs[i], sems.at[0, i]) for i in range(n)]
+    outs = [pltpu.make_async_copy(bufs[i], dsts[i], sems.at[1, i]) for i in range(n)]
+    for copy in ins:
+        copy.start()
+    for came, goes in zip(ins, outs):
+        came.wait()
+        goes.start()
+    for copy in outs:
+        copy.wait()
 
 
 def per_device(tokens, routes, kept_mask, gate_probs, output_grad, w_gate, w_up, w_down):
@@ -570,6 +645,7 @@
     wg, wu, wd = w_gate[0], w_up[0], w_down[0]
     vmem = pl.BlockSpec(memory_space=pltpu.VMEM)
     hbm = pl.BlockSpec(memory_space=pl.ANY)
+    src = pl.BlockSpec(memory_space=pltpu.HBM)
     dma = pltpu.SemaphoreType.DMA
     gather_sems = [dma((8,)), dma((2, NZ)), dma((2, NZ)), dma((4, NZ))]
     outs = pl.pallas_call(
@@ -581,8 +657,8 @@
             jax.ShapeDtypeStruct(wu.shape, BF16),
             jax.ShapeDtypeStruct(wd.shape, BF16),
         ),
-        in_specs=[hbm, hbm] + [vmem] * 6,
-        out_specs=[vmem] * 5,
+        in_specs=[src] * 8,
+        out_specs=[vmem] * 2 + [hbm] * 3,
         scratch_shapes=[
             pltpu.VMEM((NZ, tok_rows, 2 * width), BF16),
             pltpu.VMEM((NZ, 16, tok_rows), F32),
@@ -594,15 +670,27 @@
             pltpu.VMEM((NF, hid, width), BF16),
             pltpu.VMEM((NZ, CH, 2 * width), BF16),
             pltpu.VMEM((NZ, CH, 2 * width), BF16),
-            pltpu.VMEM((2, NZ // 2, tok_rows, 2 * width), BF16),
-            pltpu.VMEM((2, NZ // 2, tok_rows, 2 * width), BF16),
+            pltpu.VMEM((2, NZ // 2, 2, tok_rows, width), BF16),
+            pltpu.VMEM((2, NZ // 2, 2, tok_rows, width), BF16),
             pltpu.VMEM((CH, tok_rows), F32),
             pltpu.VMEM((NX, 16, tok_rows), F32),
-            dma((4,)),
+            pltpu.VMEM((hid, model), BF16),
+            pltpu.VMEM((model, 2 * hid), BF16),
+            pltpu.VMEM((hid, model), BF16),
+            pltpu.VMEM((8, 128), F32),
+            pltpu.VMEM((NZ, tok_rows, 2 * CH), BF16),
+            pltpu.VMEM((NZ, tok_rows, CH), BF16),
+            pltpu.VMEM((model, hid), BF16),
+            pltpu.VMEM((NF, 2 * hid, width), BF16),
+            pltpu.VMEM((8, tok_rows), jnp.int32),
+            pltpu.VMEM((8, tok_rows), jnp.int32),
+            pltpu.VMEM((8, tok_rows), F32),
+            dma((8,)),
+            dma((3,)),
             dma((3,)),
             dma((3, NF)),
             dma((2, 2)),
-            dma((2, 2, NZ // 2)),
+            dma((2, 3, NZ // 2)),
             dma(()),
             dma((NZ, NX)),
             dma(()),
@@ -612,13 +700,20 @@
             dma(()),
             dma((NZ, NX)),
             dma((2,)),
-            dma((2, NZ // 2)),
+            dma((2, NZ // 2, 2)),
         ],
         compiler_params=pltpu.CompilerParams(
-            collective_id=0, has_side_effects=True, vmem_limit_bytes=56 * 1024 * 1024
+            collective_id=0, has_side_effects=True, vmem_limit_bytes=58 * 1024 * 1024
         ),
     )(tokens, output_grad, routes.T, kept_mask.T, gate_probs.T, wg, wu, wd)
-    output, input_grad, g_gate, g_up, g_down = outs
+    output, input_grad, g_gate, g_up, g_down = pl.pallas_call(
+        functools.partial(put_out, len(outs)),
+        out_shape=tuple(jax.ShapeDtypeStruct(o.shape, o.dtype) for o in outs),
+        in_specs=[hbm] * 5,
+        out_specs=[hbm] * 5,
+        scratch_shapes=[pltpu.VMEM(o.shape, o.dtype) for o in outs] + [dma((2, 5))],
+        compiler_params=pltpu.CompilerParams(vmem_limit_bytes=58 * 1024 * 1024),
+    )(*outs)
     return output, input_grad, g_gate[None], g_up[None], g_down[None]
 
 

time: 149 us -> 135 us (0.906)
  Pallas kernels: 141 us -> 133 us
  local copies, waits for them, and re-layouts: 6.09 us -> 0 us
    pallas_call x1, Pallas kernels: 141 us -> 131 us  [per_device(): pl.pallas_call(kernel, out_shape=(jax.ShapeDtypeStruct((tok_rows, width),...]
    unnamed x11 -> x0, local copies, waits for them, and re-layouts: 6.09 us -> none
    pallas_call x0 -> x1, Pallas kernels: none -> 2.35 us  [per_device(): pl.pallas_call(functools.partial(put_out, len(outs)), out_shape=tuple((ja...]
where the time goes in v2:
time: 135 us; the launch traced here: 134 us
  Pallas kernels  133 us (99%)
    pallas_call x1, Pallas kernels, per_device(): pl.pallas_call(kernel, out_shape=(jax.ShapeDtypeStruct((tok_rows, width),...  131 us

profile of v2, /device:TPU:6, one launch (start us, length us, event | category | flops | bytes accessed | tf_op | source)
XLA Modules:
  0.0 134.0 jit_solution(13284063182170457133)
XLA Ops:
  0.6 131.1 %shard_map.119 = (bf16[128,256]{1,0:T(8,128)(2,1)}, bf16[128,256]{1,0:T(8,128)(2,1)}, bf16[2048,128]{1,0:T(8,128)(2,1)}, bf16[2048,128]{1,0:T(8,128)(2,1)}, bf16[128,2048]{1,0:T(8,128)(2,1)}) custom-call(bf16[128,2048]{1,0:T(8,128)(2,1)} %tok.1, bf16[128,2048]{1,0:T(8,128)(2,1)} %grd.1, s32[8,128]{1,0:T(8,128)} %bitcast.12, s32[8,128]{1,0:T(8,128)} %bitcast.13, ...), custom_call_target="tpu_custom_call" | custom-call | tf_op jit(solution)/shard_map/pallas_call | solution.py:651
  131.7 2.3 %shard_map.120 = (bf16[128,256]{1,0:T(8,128)(2,1)}, bf16[128,256]{1,0:T(8,128)(2,1)}, bf16[2048,128]{1,0:T(8,128)(2,1)}, bf16[2048,128]{1,0:T(8,128)(2,1)}, bf16[128,2048]{1,0:T(8,128)(2,1)}) custom-call(bf16[128,256]{1,0:T(8,128)(2,1)} %get-tuple-element.15.refs_0_, bf16[128,256]{1,0:T(8,128)(2,1)} %get-tuple-element.16.refs_1_, ...), custom_call_target="tpu_custom_call" | custom-call | tf_op jit(solution)/shard_map/pallas_call | solution.py:709

commit v3 on v2

--- a/solution.py
+++ b/solution.py
@@ -17,6 +17,9 @@
 CH = 64
 LAG = 4
 EARLY = 1
+EARLY_W = (0, 1)
+LATE_W = (2,)
+LATE = 10
 TN = (((0,), (0,)), ((), ()))
 
 
@@ -110,6 +113,7 @@
     yp, ym, y2 = mod(y + 1, NY), mod(y - 1, NY), mod(y + 2, NY)
     oc = 1 - c
     width = out.shape[1]
+    tok_rows = routes.shape[1]
 
     cols = pl.ds(pl.multiple_of(f * width, width), width)
     own_t = pltpu.make_async_copy(tok.at[:, cols], tbuf.at[z, :, pl.ds(0, width)], local_sem.at[0])
@@ -140,8 +144,65 @@
             barrier, inc=1, device_id={"y": to // NC, "c": lax.rem(to, NC)}, device_id_type=MESH
         )
 
+    pl.semaphore_wait(barrier, 2 + (NX - 1) + (NF - 1))
+    own_t.wait()
+    own_g.wait()
+
+    def z_copies(direction, s, hop):
+        to = zp if direction == 0 else zm
+        half = tok_rows // 2
+        parts = [rbuf.at[s]] + [tbuf.at[s, pl.ds(i * half, half), :] for i in range(2)]
+        return [
+            rdma(part, part, z_send.at[direction, min(i, 1)], z_recv.at[direction, i, hop], z=to)
+            for i, part in enumerate(parts)
+        ]
+
+    def z_pass(direction, s, hop, onward, which):
+        arrived = z_copies(direction, s, hop)
+        following = z_copies(direction, s, hop + 1)
+        for came, goes in zip(arrived[which], following[which]):
+            came.wait_recv()
+
+            @pl.when(onward)
+            def _():
+                goes.start()
+
+    for direction in range(2):
+        for copy in z_copies(direction, z, 0)[1:]:
+            copy.start()
+
+    def wblock(ref, b):
+        at = pl.ds(pl.multiple_of(b * width, width), width)
+        return ref.at[at, :] if ref is not wd else ref.at[:, at]
+
+    def wplace(i, b):
+        return (
+            gu.at[b, :, pl.ds(0, hid)] if i == 0 else gu.at[b, :, pl.ds(hid, hid)] if i == 1 else dn.at[b]
+        )
+
+    def weights_send(d, kinds):
+        to = mod(f + d, NF)
+        for i in kinds:
+            ref = (wg, wu, wd)[i]
+            rdma(
+                wblock(ref, to),
+                wplace(i, f),
+                wgt_send.at[i],
+                wgt_recv.at[i, f],
+                y=to // NC,
+                c=lax.rem(to, NC),
+            ).start()
+
+    for d in range(1, NF):
+        weights_send(d, EARLY_W)
+    own_w = [
+        pltpu.make_async_copy(wblock(ref, f), wplace(i, f), wgt_recv.at[i, f])
+        for i, ref in enumerate((wg, wu, wd))
+    ]
+    for copy in own_w:
+        copy.start()
+
     nexp = NX * NZ
-    tok_rows = routes.shape[1]
     for copy in infos:
         copy.wait()
     rt = routes[...]
@@ -164,62 +225,8 @@
         rbuf[z, 8 + k : 9 + k, :] = weight[k : k + 1, :]
     cst[...] = jnp.zeros_like(cst)
 
-    pl.semaphore_wait(barrier, 2 + (NX - 1) + (NF - 1))
-    own_t.wait()
-    own_g.wait()
-
-    def z_copies(direction, s, hop):
-        to = zp if direction == 0 else zm
-        half = tok_rows // 2
-        parts = [rbuf.at[s]] + [tbuf.at[s, pl.ds(i * half, half), :] for i in range(2)]
-        return [
-            rdma(part, part, z_send.at[direction, min(i, 1)], z_recv.at[direction, i, hop], z=to)
-            for i, part in enumerate(parts)
-        ]
-
-    def z_start(direction, s, hop):
-        for copy in z_copies(direction, s, hop):
-            copy.start()
-
-    def z_pass(direction, s, hop, onward, which):
-        arrived = z_copies(direction, s, hop)
-        following = z_copies(direction, s, hop + 1)
-        for came, goes in zip(arrived[which], following[which]):
-            came.wait_recv()
-
-            @pl.when(onward)
-            def _():
-                goes.start()
-
-    z_start(0, z, 0)
-    z_start(1, z, 0)
-
-    def wblock(ref, b):
-        at = pl.ds(pl.multiple_of(b * width, width), width)
-        return ref.at[at, :] if ref is not wd else ref.at[:, at]
-
-    def wplace(i, b):
-        return (
-            gu.at[b, :, pl.ds(0, hid)] if i == 0 else gu.at[b, :, pl.ds(hid, hid)] if i == 1 else dn.at[b]
-        )
-
-    for d in range(1, NF):
-        to = mod(f + d, NF)
-        for i, ref in enumerate((wg, wu, wd)):
-            rdma(
-                wblock(ref, to),
-                wplace(i, f),
-                wgt_send.at[i],
-                wgt_recv.at[i, f],
-                y=to // NC,
-                c=lax.rem(to, NC),
-            ).start()
-    own_w = [
-        pltpu.make_async_copy(wblock(ref, f), wplace(i, f), wgt_recv.at[i, f])
-        for i, ref in enumerate((wg, wu, wd))
-    ]
-    for copy in own_w:
-        copy.start()
+    for direction in range(2):
+        z_copies(direction, z, 0)[0].start()
 
     def selection(s):
         info = rbuf[s]
@@ -350,12 +357,13 @@
 
     half_ring = NZ // 2
 
-    def weights_wait():
-        for copy in own_w:
-            copy.wait()
+    def weights_wait(kinds):
+        for i in kinds:
+            own_w[i].wait()
         for d in range(1, NF):
             frm = mod(f + d, NF)
-            for i, ref in enumerate((wg, wu, wd)):
+            for i in kinds:
+                ref = (wg, wu, wd)[i]
                 rdma(
                     wblock(ref, frm),
                     wplace(i, frm),
@@ -396,6 +404,11 @@
 
         z_step(slice(2, 3))
 
+        @pl.when(i == LATE)
+        def _():
+            for d in range(1, NF):
+                weights_send(d, LATE_W)
+
         @pl.when(i < half_ring)
         def _():
             select_rows(sa)
@@ -410,7 +423,7 @@
 
         @pl.when(i == half_ring)
         def _():
-            weights_wait()
+            weights_wait(EARLY_W)
 
         @pl.when(i >= half_ring)
         def _():
@@ -480,31 +493,35 @@
             pick_o[s], jnp.concatenate([back, back], axis=0), preferred_element_type=F32
         )
 
-    def p_copy(direction, kind, m):
+    halves = [pl.ds(i * (tok_rows // 2), tok_rows // 2) for i in range(2)]
+
+    def p_copy(direction, kind, m, h):
         to = zp if direction == 0 else zm
         return rdma(
-            psend.at[direction, m, kind],
-            precv.at[direction, m, kind],
+            psend.at[direction, m, kind, halves[h], :],
+            precv.at[direction, m, kind, halves[h], :],
             p_send.at[direction],
-            p_recv.at[direction, m, kind],
+            p_recv.at[direction, m, 2 * kind + h],
             z=to,
         )
 
     def pass_on(direction, kind, s, m):
         part = share(kind, s)
-
-        @pl.when(m == 0)
-        def _():
-            psend[direction, m, kind] = part.astype(BF16)
-
-        @pl.when(m >= 1)
-        def _():
-            before_m = jnp.maximum(m - 1, 0)
-            p_copy(direction, kind, before_m).wait_recv()
-            came = precv[direction, before_m, kind].astype(F32)
-            psend[direction, m, kind] = (part + came).astype(BF16)
-
-        p_copy(direction, kind, m).start()
+        for h in range(2):
+            mine = part[h * (tok_rows // 2) : (h + 1) * (tok_rows // 2)]
+
+            @pl.when(m == 0)
+            def _():
+                psend[direction, m, kind, halves[h], :] = mine.astype(BF16)
+
+            @pl.when(m >= 1)
+            def _():
+                before_m = jnp.maximum(m - 1, 0)
+                p_copy(direction, kind, before_m, h).wait_recv()
+                came = precv[direction, before_m, kind, halves[h], :].astype(F32)
+                psend[direction, m, kind, halves[h], :] = (mine + came).astype(BF16)
+
+            p_copy(direction, kind, m, h).start()
 
     def grad_out(b):
         at = pl.ds(pl.multiple_of(b * width, width), width)
@@ -550,6 +567,10 @@
             for s in back_pair(i):
                 forward2(s)
 
+        @pl.when(i == 2)
+        def _():
+            weights_wait(LATE_W)
+
         @pl.when(i >= 2)
         def _():
             chunks = back_pair(i - 2)
@@ -594,9 +615,11 @@
     x_waits(eo_src, ret_dst, e_send, e_recv, sb)
     for kind, ref in enumerate((out, ing)):
         part = share(kind, sb)
-        p_copy(1, kind, last - 1).wait_recv()
+        for h in range(2):
+            p_copy(1, kind, last - 1, h).wait_recv()
         part += precv[1, last - 1, kind].astype(F32)
-        p_copy(0, kind, last).wait_recv()
+        for h in range(2):
+            p_copy(0, kind, last, h).wait_recv()
         ref[...] = (part + precv[0, last, kind].astype(F32)).astype(BF16)
 
     drain1()
@@ -700,7 +723,7 @@
             dma(()),
             dma((NZ, NX)),
             dma((2,)),
-            dma((2, NZ // 2, 2)),
+            dma((2, NZ // 2, 4)),
         ],
         compiler_params=pltpu.CompilerParams(
             collective_id=0, has_side_effects=True, vmem_limit_bytes=58 * 1024 * 1024

time: 135 us -> 131 us (0.970)
  Pallas kernels: 133 us -> 130 us
    pallas_call x1, Pallas kernels: 131 us -> 128 us  [per_device(): pl.pallas_call(kernel, out_shape=(jax.ShapeDtypeStruct((tok_rows, width),...]
where the time goes in v3:
time: 131 us
  Pallas kernels  130 us (99%)
    pallas_call x1, Pallas kernels, per_device(): pl.pallas_call(kernel, out_shape=(jax.ShapeDtypeStruct((tok_rows, width),...  128 us

profile of v3, /device:TPU:6, one launch (start us, length us, event | category | flops | bytes accessed | tf_op | source)
XLA Modules:
  0.0 130.7 jit_solution(12219853785343437707)
XLA Ops:
  0.6 127.7 %shard_map.119 = (bf16[128,256]{1,0:T(8,128)(2,1)}, bf16[128,256]{1,0:T(8,128)(2,1)}, bf16[2048,128]{1,0:T(8,128)(2,1)}, bf16[2048,128]{1,0:T(8,128)(2,1)}, bf16[128,2048]{1,0:T(8,128)(2,1)}) custom-call(bf16[128,2048]{1,0:T(8,128)(2,1)} %tok.1, bf16[128,2048]{1,0:T(8,128)(2,1)} %grd.1, s32[8,128]{1,0:T(8,128)} %bitcast.12, s32[8,128]{1,0:T(8,128)} %bitcast.13, ...), custom_call_target="tpu_custom_call" | custom-call | tf_op jit(solution)/shard_map/pallas_call | solution.py:674
  128.4 2.3 %shard_map.120 = (bf16[128,256]{1,0:T(8,128)(2,1)}, bf16[128,256]{1,0:T(8,128)(2,1)}, bf16[2048,128]{1,0:T(8,128)(2,1)}, bf16[2048,128]{1,0:T(8,128)(2,1)}, bf16[128,2048]{1,0:T(8,128)(2,1)}) custom-call(bf16[128,256]{1,0:T(8,128)(2,1)} %get-tuple-element.15.refs_0_, bf16[128,256]{1,0:T(8,128)(2,1)} %get-tuple-element.16.refs_1_, ...), custom_call_target="tpu_custom_call" | custom-call | tf_op jit(solution)/shard_map/pallas_call | solution.py:732
